TPU v7x, 32 devices: a whole 2x2x4 slice. The times are simulated.
32 devices in a mesh: groups: 2 (over x), seq: 16 (over z, y, core).
Axes of the slice: x: 2, y: 2, z: 4, core: 2. Of those that a mesh axis runs over, the one named last changes fastest.
Arguments:
- sequence: bfloat16 [8192, 1536], P(('groups', 'seq')), parts along dimension 0, may hold values from -6 to 6
- gain_conv: float32 [1536], replicated, may hold values from 0.25 to 1.75
- conv_weight: float32 [5, 1536], replicated, may hold values from -3 to 3
- gain_attn: float32 [1536], replicated, may hold values from 0.25 to 1.75
- w_query: bfloat16 [1536, 1024], replicated
- w_key: bfloat16 [1536, 128], replicated
- w_value: bfloat16 [1536, 192], replicated, may hold values from -0.15625 to 0.15625
- w_out: bfloat16 [1536, 1536], replicated, may hold values from -0.15625 to 0.15625
- w_left: bfloat16 [1536, 128], replicated, may hold values from -0.15625 to 0.15625
- w_right: bfloat16 [1536, 128], replicated, may hold values from -0.15625 to 0.15625
- w_pair: bfloat16 [3, 3, 128, 128], replicated, may hold values from -0.1875 to 0.1875
Outputs:
- track: bfloat16 [8192, 1536], P(('groups', 'seq')), parts along dimension 0
- pair_map: bfloat16 [512, 256, 128], P(('groups', 'seq')), parts along dimension 0
There are 2 independent parts, one for each index of `groups`. A program takes and returns all parts, laid end to end along the dimension named above; an argument that names none is the same for every part. Nothing has to cross between parts.
All inputs are finite; a program needn't handle non-finite values.
Results may differ from a plain program's by a relative error of at most 0.019.
Values may be sent and summed in bfloat16 or wider, within the bound.
A program may use at most 128 MiB of HBM per device.

v0:
```python
import jax
import jax.numpy as jnp
from jax import lax
from jax.sharding import PartitionSpec as P

HEADS = 8
POOL = 16


def extended_2(cells, sides, width):
    for axis, dim in sides:
        count = lax.axis_size(axis)
        ends = count - 1
        head = lax.slice_in_dim(cells, 0, width, axis=dim)
        tail = lax.slice_in_dim(cells, cells.shape[dim] - width, cells.shape[dim], axis=dim)
        cells = jnp.concatenate(
            [
                lax.ppermute(tail, axis, [(i, (i + 1) % count) for i in range(ends)]),
                cells,
                lax.ppermute(head, axis, [((i + 1) % count, i) for i in range(ends)]),
            ],
            axis=dim,
        )
    return cells


def rms_norm(values, gain):
    values = values.astype(jnp.float32)
    scale = lax.rsqrt(jnp.mean(values * values, axis=-1, keepdims=True) + 1e-06)
    return values * scale * gain


def attend_block(carry, queries, keys_part, values_part):
    running, totals, numer = carry
    scale = 1.0 / jnp.sqrt(jnp.float32(queries.shape[2]))
    scores = (
        jnp.einsum("qhd,kd->hqk", queries, keys_part, preferred_element_type=jnp.float32) * scale
    )
    newtop = jnp.maximum(running, jnp.max(scores, axis=-1))
    expo = jnp.exp(scores - newtop[..., None])
    factor = jnp.exp(running - newtop)
    totals = totals * factor + jnp.sum(expo, axis=-1)
    numer = numer * factor[..., None] + jnp.einsum(
        "hqk,kv->hqv", expo.astype(jnp.bfloat16), values_part, preferred_element_type=jnp.float32
    )
    return (newtop, totals, numer)


def attend_piece(carry, queries, keys_part, values_part):
    length = keys_part.shape[0]
    key_blocks = keys_part.reshape(length // 512, 512, keys_part.shape[1])
    value_blocks = values_part.reshape(length // 512, 512, values_part.shape[1])

    def stepper(state, blocks):
        return (attend_block(state, queries, blocks[0], blocks[1]), None)

    carry, unused = lax.scan(stepper, carry, (key_blocks, value_blocks))
    return carry


def local(
    sequence,
    gain_conv,
    conv_weight,
    gain_attn,
    w_query,
    w_key,
    w_value,
    w_out,
    w_left,
    w_right,
    w_pair,
):
    rows = sequence.shape[0]
    width = sequence.shape[1]
    heads = HEADS
    key_size = w_key.shape[1]
    value_size = w_value.shape[1]
    normed = rms_norm(sequence, gain_conv).astype(jnp.bfloat16)
    padded = extended_2(normed, (("seq", 0),), 2)
    convolved = jnp.zeros((rows, width), jnp.float32)
    for offset in range(conv_weight.shape[0]):
        convolved = convolved + conv_weight[offset][None, :] * padded[
            offset : offset + rows
        ].astype(jnp.float32)
    first = (sequence.astype(jnp.float32) + convolved).astype(jnp.bfloat16)
    attn_in = rms_norm(first, gain_attn).astype(jnp.bfloat16)
    queries = (
        jnp.dot(attn_in, w_query, preferred_element_type=jnp.float32)
        .astype(jnp.bfloat16)
        .reshape(rows, heads, key_size)
    )
    initial = (
        jnp.full((heads, rows), -1e30, jnp.float32),
        jnp.zeros((heads, rows), jnp.float32),
        jnp.zeros((heads, rows, value_size), jnp.float32),
    )
    keys_local = jnp.dot(attn_in, w_key, preferred_element_type=jnp.float32).astype(jnp.bfloat16)
    values_local = jnp.dot(attn_in, w_value, preferred_element_type=jnp.float32).astype(
        jnp.bfloat16
    )
    running, totals, numer = attend_piece(
        initial,
        queries,
        lax.all_gather(keys_local, "seq", axis=0, tiled=True),
        lax.all_gather(values_local, "seq", axis=0, tiled=True),
    )
    result = numer / totals[..., None]
    attended = (
        jnp.transpose(result, (1, 0, 2)).reshape(rows, heads * value_size).astype(jnp.bfloat16)
    )
    track = (
        first.astype(jnp.float32) + jnp.dot(attended, w_out, preferred_element_type=jnp.float32)
    ).astype(jnp.bfloat16)
    pooled = jnp.mean(track.astype(jnp.float32).reshape(rows // POOL, POOL, width), axis=1).astype(
        jnp.bfloat16
    )
    left = jnp.dot(pooled, w_left, preferred_element_type=jnp.float32).astype(jnp.bfloat16)
    right = jnp.dot(pooled, w_right, preferred_element_type=jnp.float32).astype(jnp.bfloat16)
    band = left.shape[0]
    right_all = lax.all_gather(right, "seq", axis=0, tiled=True)
    pair0 = (
        left.astype(jnp.float32)[:, None, :] * right_all.astype(jnp.float32)[None, :, :]
    ).astype(jnp.bfloat16)
    activated = jax.nn.gelu(pair0.astype(jnp.float32)).astype(jnp.bfloat16)
    extended = extended_2(activated, (("seq", 0),), 1)
    columns = right_all.shape[0]
    channels = right_all.shape[1]
    grid = jnp.pad(extended, ((0, 0), (1, 1), (0, 0)))
    summed = jnp.zeros((band * columns, channels), jnp.float32)
    for row_off in range(3):
        for col_off in range(3):
            window = grid[row_off : row_off + band, col_off : col_off + columns].reshape(
                band * columns, channels
            )
            summed = summed + jnp.dot(
                window, w_pair[row_off, col_off], preferred_element_type=jnp.float32
            )
    pair_map = (pair0.astype(jnp.float32) + summed.reshape(band, columns, channels)).astype(
        jnp.bfloat16
    )
    return (track, pair_map)


def solution(mesh):
    placed = (P(("groups", "seq"), None), P(), P(), P(), P(), P(), P(), P(), P(), P(), P())
    return jax.shard_map(
        local,
        mesh=mesh,
        in_specs=placed,
        out_specs=(P(("groups", "seq"), None), P(("groups", "seq"), None, None)),
        check_vma=False,
    )
```

profile of v0, /device:TPU:1, one launch (start us, length us, event | category | flops | bytes accessed | tf_op | source)
XLA Modules:
  0.0 204.6 jit_solution(1153907717193346455)
XLA Ops:
  7.2 1.5 fusion.29
  8.8 1.4 fusion.31
  10.3 4.5 %collective-permute-start = (bf16[2,1536]{1,0:T(2,128)(2,1)S(1)}, bf16[2,1536]{1,0:T(2,128)(2,1)S(1)}, u32[]{:S(2)}, u32[]{:S(2)}) collective-permute-start(bf16[2,1536]{1,0:T(2,128)(2,1)S(1)} %get-tuple-element.108), channel_id=1, source_target_pairs={{0,1},{1,2},{2,3},{3,4},{4,5},{5,6},{6,7},{7,8},{8,9},{9,10},{10,1... | collective-permute-start | bytes 18440 | tf_op jit(solution)/shard_map/ppermute | solution.py:18
  14.8 1.9 collective-permute-start.1
  16.8 2.9 %collective-permute-done.1 = bf16[2,1536]{1,0:T(2,128)(2,1)S(1)} collective-permute-done((bf16[2,1536]{1,0:T(2,128)(2,1)S(1)}, bf16[2,1536]{1,0:T(2,128)(2,1)S(1)}, u32[]{:S(2)}, u32[]{:S(2)}) %collective-permute-start.1) | collective-permute-done | bytes 6176 | tf_op jit(solution)/shard_map/ppermute | solution.py:20
  19.7 1.6 fusion.33
  21.3 0.9 copy-done.4
  22.2 1.1 convolution_convert_fusion.1
  23.4 2.3 %convolution_convert_fusion.2 = bf16[256,128]{1,0:T(8,128)(2,1)} fusion(bf16[1536,128]{1,0:T(8,128)(2,1)} %param.18, bf16[256,1536]{1,0:T(8,128)(2,1)} %copy-done.4, f32[1536]{0:T(1024)S(1)} %copy-done.11, f32[256]{0:T(256)S(1)} %add_rsqrt_fusion), kind=kOutput, calls=%fused_computation.71 | convolution fusion | flops 102268928 | bytes 1252352 | tf_op jit(solution)/shard_map/dot_general | solution.py:98
  25.7 2.2 %fusion.39 = bf16[32,8,8,128]{3,2,1,0:T(8,128)(2,1)S(1)} fusion(bf16[1536,1024]{1,0:T(8,128)(2,1)S(1)} %copy-done, bf16[256,1536]{1,0:T(8,128)(2,1)} %copy-done.4, f32[1536]{0:T(1024)S(1)} %copy-done.11, f32[256]{0:T(256)S(1)} %add_rsqrt_fusion), kind=kOutput, calls=%fused_computation.67 | convolution fusion | flops 807141376 | bytes 4463616 | tf_op jit(solution)/shard_map/dot_general | solution.py:89
  27.9 0.9 copy.22
  28.8 34.5 %all-gather.5.cloned.1.call-done = bf16[4096,192]{0,1:T(8,128)(2,1)} async-done(((bf16[256,192]{0,1:T(8,128)(2,1)}), bf16[4096,192]{0,1:T(8,128)(2,1)}) %all-gather.5.cloned.1.call-update) | async-done | bytes 1572880 | tf_op jit(solution)/shard_map/all_gather | solution.py:106
  63.3 2.7 %copy.21 = bf16[24,8,8,512]{3,2,0,1:T(8,128)(2,1)} copy(bf16[24,8,8,512]{3,2,1,0:T(8,128)(2,1)} %bitcast.116) | data formatting | bytes 3145728 | tf_op jit(solution)/shard_map/reshape | solution.py:52
  66.0 36.7 %all-gather.3.cloned.1.call-done = bf16[4096,128]{1,0:T(8,128)(2,1)} async-done(((bf16[256,128]{1,0:T(8,128)(2,1)}), bf16[4096,128]{1,0:T(8,128)(2,1)}) %all-gather.3.cloned.1.call-update) | async-done | bytes 1048592 | tf_op jit(solution)/shard_map/all_gather | solution.py:105
  102.7 53.1 %while.15 = (s32[]{:T(128)}, f32[8,256]{1,0:T(8,128)S(1)}, f32[8,256]{1,0:T(8,128)S(1)}, f32[8,256,192]{1,2,0:T(8,128)}, bf16[8,512,128]{2,1,0:T(8,128)(2,1)}, /...) while((s32[]{:T(128)}, f32[8,256]{1,0:T(8,128)S(1)}, ...), condition=%wide.region_5.6_spmd.clone, body=%wide.region_2.5_spmd.clone.sunk | while | flops 680667136 | bytes 29294768 | solution.py:57
  102.7 1.8 bitcast_reduce_fusion.2
  106.0 2.2 %fusion.102 = f32[8,256,192]{1,2,0:T(8,128)S(1)} fusion(f32[8,256,192]{1,2,0:T(8,128)S(1)} %copy-done.1, f32[512,256,8]{1,0,2:T(8,128)S(1)} %get-tuple-element.160, f32[8,256]{1,0:T(8,128)S(1)} %select_maximum_fusion.2, f32[8,256]{1,0:T(8,128)S(1)} %get-tuple-element.162, pred[]{:T(512)S(6)} %compare.44, ...), kind=kOutput, calls=%fused_computation.9.clone.1 | convolution fusion | flops 406978560 | bytes 7553029 | tf_op jit(solution)/shard_map/while/body/eval_jaxpr/hqk,kv->hqv/dot_general | solution.py:43
  108.2 1.1 copy-done.2
  109.4 1.8 bitcast_reduce_fusion.2
  112.6 2.2 %fusion.102 = f32[8,256,192]{1,2,0:T(8,128)S(1)} fusion(f32[8,256,192]{1,2,0:T(8,128)S(1)} %copy-done.1, f32[512,256,8]{1,0,2:T(8,128)S(1)} %get-tuple-element.160, f32[8,256]{1,0:T(8,128)S(1)} %select_maximum_fusion.2, f32[8,256]{1,0:T(8,128)S(1)} %get-tuple-element.162, pred[]{:T(512)S(6)} %compare.44, ...), kind=kOutput, calls=%fused_computation.9.clone.1 | convolution fusion | flops 406978560 | bytes 7553029 | tf_op jit(solution)/shard_map/while/body/eval_jaxpr/hqk,kv->hqv/dot_general | solution.py:43
  114.9 1.1 copy-done.2
  116.0 1.8 bitcast_reduce_fusion.2
  119.3 2.2 %fusion.102 = f32[8,256,192]{1,2,0:T(8,128)S(1)} fusion(f32[8,256,192]{1,2,0:T(8,128)S(1)} %copy-done.1, f32[512,256,8]{1,0,2:T(8,128)S(1)} %get-tuple-element.160, f32[8,256]{1,0:T(8,128)S(1)} %select_maximum_fusion.2, f32[8,256]{1,0:T(8,128)S(1)} %get-tuple-element.162, pred[]{:T(512)S(6)} %compare.44, ...), kind=kOutput, calls=%fused_computation.9.clone.1 | convolution fusion | flops 406978560 | bytes 7553029 | tf_op jit(solution)/shard_map/while/body/eval_jaxpr/hqk,kv->hqv/dot_general | solution.py:43
  121.5 1.1 copy-done.2
  122.6 1.8 bitcast_reduce_fusion.2
  125.9 2.2 %fusion.102 = f32[8,256,192]{1,2,0:T(8,128)S(1)} fusion(f32[8,256,192]{1,2,0:T(8,128)S(1)} %copy-done.1, f32[512,256,8]{1,0,2:T(8,128)S(1)} %get-tuple-element.160, f32[8,256]{1,0:T(8,128)S(1)} %select_maximum_fusion.2, f32[8,256]{1,0:T(8,128)S(1)} %get-tuple-element.162, pred[]{:T(512)S(6)} %compare.44, ...), kind=kOutput, calls=%fused_computation.9.clone.1 | convolution fusion | flops 406978560 | bytes 7553029 | tf_op jit(solution)/shard_map/while/body/eval_jaxpr/hqk,kv->hqv/dot_general | solution.py:43
  128.1 1.1 copy-done.2
  129.3 1.8 bitcast_reduce_fusion.2
  132.5 2.2 %fusion.102 = f32[8,256,192]{1,2,0:T(8,128)S(1)} fusion(f32[8,256,192]{1,2,0:T(8,128)S(1)} %copy-done.1, f32[512,256,8]{1,0,2:T(8,128)S(1)} %get-tuple-element.160, f32[8,256]{1,0:T(8,128)S(1)} %select_maximum_fusion.2, f32[8,256]{1,0:T(8,128)S(1)} %get-tuple-element.162, pred[]{:T(512)S(6)} %compare.44, ...), kind=kOutput, calls=%fused_computation.9.clone.1 | convolution fusion | flops 406978560 | bytes 7553029 | tf_op jit(solution)/shard_map/while/body/eval_jaxpr/hqk,kv->hqv/dot_general | solution.py:43
  134.8 1.1 copy-done.2
  135.9 1.8 bitcast_reduce_fusion.2
  139.2 2.2 %fusion.102 = f32[8,256,192]{1,2,0:T(8,128)S(1)} fusion(f32[8,256,192]{1,2,0:T(8,128)S(1)} %copy-done.1, f32[512,256,8]{1,0,2:T(8,128)S(1)} %get-tuple-element.160, f32[8,256]{1,0:T(8,128)S(1)} %select_maximum_fusion.2, f32[8,256]{1,0:T(8,128)S(1)} %get-tuple-element.162, pred[]{:T(512)S(6)} %compare.44, ...), kind=kOutput, calls=%fused_computation.9.clone.1 | convolution fusion | flops 406978560 | bytes 7553029 | tf_op jit(solution)/shard_map/while/body/eval_jaxpr/hqk,kv->hqv/dot_general | solution.py:43
  141.4 1.1 copy-done.2
  142.5 1.8 bitcast_reduce_fusion.2
  145.8 2.2 %fusion.102 = f32[8,256,192]{1,2,0:T(8,128)S(1)} fusion(f32[8,256,192]{1,2,0:T(8,128)S(1)} %copy-done.1, f32[512,256,8]{1,0,2:T(8,128)S(1)} %get-tuple-element.160, f32[8,256]{1,0:T(8,128)S(1)} %select_maximum_fusion.2, f32[8,256]{1,0:T(8,128)S(1)} %get-tuple-element.162, pred[]{:T(512)S(6)} %compare.44, ...), kind=kOutput, calls=%fused_computation.9.clone.1 | convolution fusion | flops 406978560 | bytes 7553029 | tf_op jit(solution)/shard_map/while/body/eval_jaxpr/hqk,kv->hqv/dot_general | solution.py:43
  148.0 1.1 copy-done.2
  149.2 1.8 bitcast_reduce_fusion.2
  152.4 2.2 %fusion.102 = f32[8,256,192]{1,2,0:T(8,128)S(1)} fusion(f32[8,256,192]{1,2,0:T(8,128)S(1)} %copy-done.1, f32[512,256,8]{1,0,2:T(8,128)S(1)} %get-tuple-element.160, f32[8,256]{1,0:T(8,128)S(1)} %select_maximum_fusion.2, f32[8,256]{1,0:T(8,128)S(1)} %get-tuple-element.162, pred[]{:T(512)S(6)} %compare.44, ...), kind=kOutput, calls=%fused_computation.9.clone.1 | convolution fusion | flops 406978560 | bytes 7553029 | tf_op jit(solution)/shard_map/while/body/eval_jaxpr/hqk,kv->hqv/dot_general | solution.py:43
  154.7 1.1 copy-done.2
  155.8 1.6 divide_convert_fusion
  157.5 4.8 %convert_reduce_fusion = (f32[16,1536]{1,0:T(8,128)S(1)}, bf16[256,1536]{1,0:T(8,128)(2,1)}) fusion(bf16[256,1536]{0,1:T(8,128)(2,1)S(1)} %bitcast.117, bf16[1536,1536]{1,0:T(8,128)(2,1)} %param.20, bf16[256,1536]{1,0:T(8,128)(2,1)S(1)} %copy-done.5), kind=kOutput, calls=%fused_computation.61 | convolution fusion | flops 1209901056 | bytes 7176192 | tf_op jit(solution)/shard_map/dot_general | solution.py:113
  162.6 19.7 %all_gather.11 = bf16[256,128]{1,0:T(8,128)(2,1)S(1)} all-gather(bf16[16,128]{1,0:T(8,128)(2,1)S(1)} %convolution_convert_fusion.3), channel_id=1, replica_groups=mesh['groups'=2,'seq'=16] {'seq'}, dimensions={0}, use_global_device_ids=true | all-gather | bytes 69632 | tf_op jit(solution)/shard_map/all_gather | solution.py:121
  182.3 0.8 fusion.27
  183.1 1.9 collective-permute-start.2
  185.0 2.6 %collective-permute-start.3 = (bf16[1,256,128]{2,1,0:T(8,128)(2,1)S(1)}, bf16[1,256,128]{2,1,0:T(8,128)(2,1)S(1)}, u32[]{:S(2)}, u32[]{:S(2)}) collective-permute-start(bf16[1,256,128]{2,1,0:T(8,128)(2,1)S(1)} %get-tuple-element.107), channel_id=1, source_target_pairs={{1,0},{2,1},{3,2},{4,3},{5,4},{6,5},{7,6},{8,7},{9,8},{10,9},{11,1... | collective-permute-start | bytes 196616 | tf_op jit(solution)/shard_map/ppermute | solution.py:20
  187.6 3.0 %collective-permute-done.3 = bf16[1,256,128]{2,1,0:T(8,128)(2,1)S(1)} collective-permute-done((bf16[1,256,128]{2,1,0:T(8,128)(2,1)S(1)}, bf16[1,256,128]{2,1,0:T(8,128)(2,1)S(1)}, u32[]{:S(2)}, u32[]{:S(2)}) %collective-permute-start.3) | collective-permute-done | bytes 65568 | tf_op jit(solution)/shard_map/ppermute | solution.py:20
  191.0 1.5 fusion.71
  196.5 1.3 fusion.28
  (103 shorter events, 16.1 us)
Async XLA Ops:
  7.2 18.6 %copy-start = (bf16[1536,1024]{1,0:T(8,128)(2,1)S(1)}, bf16[1536,1024]{1,0:T(8,128)(2,1)}, u32[]{:S(2)}) copy-start(bf16[1536,1024]{1,0:T(8,128)(2,1)} %param.17) | copy-start | bytes 9437188
  7.2 9.5 %copy-start.9 = (f32[5,1536]{1,0:T(8,128)S(1)}, f32[5,1536]{1,0:T(8,128)}, u32[]{:S(2)}) copy-start(f32[5,1536]{1,0:T(8,128)} %param.15) | copy-start | bytes 92164
  7.2 56.1 %all-gather.5.cloned.1.call-start = ((), (), s32[]{:S(2)}) async-start(), calls=%async_computation.1 | async-start | bytes 1671168 | tf_op jit(solution)/shard_map/all_gather | solution.py:106
  7.2 12.5 %copy-start.3 = (bf16[256,1536]{1,0:T(8,128)(2,1)S(1)}, bf16[256,1536]{1,0:T(8,128)(2,1)}, u32[]{:S(2)}) copy-start(bf16[256,1536]{1,0:T(8,128)(2,1)} %param.13) | copy-start | bytes 2359300
  8.8 13.4 %copy-start.10 = (bf16[1536,192]{0,1:T(8,128)(2,1)S(1)}, bf16[1536,192]{0,1:T(8,128)(2,1)}, u32[]{:S(2)}) copy-start(bf16[1536,192]{0,1:T(8,128)(2,1)} %param.19) | copy-start | bytes 1769476
  8.8 13.4 %copy-start.11 = (f32[1536]{0:T(1024)S(1)}, f32[1536]{0:T(1024)}, u32[]{:S(2)}) copy-start(f32[1536]{0:T(1024)} %param.16) | copy-start | bytes 18436
  10.3 6.6 %collective-permute-start = (bf16[2,1536]{1,0:T(2,128)(2,1)S(1)}, bf16[2,1536]{1,0:T(2,128)(2,1)S(1)}, u32[]{:S(2)}, u32[]{:S(2)}) collective-permute-start(bf16[2,1536]{1,0:T(2,128)(2,1)S(1)} %get-tuple-element.108), channel_id=1, source_target_pairs={{0,1},{1,2},{2,3},{3,4},{4,5},{5,6},{6,7},{7,8},{8,9},{9,10},{10,1... | collective-permute-start | bytes 18440 | tf_op jit(solution)/shard_map/ppermute | solution.py:18
  14.8 4.9 %collective-permute-start.1 = (bf16[2,1536]{1,0:T(2,128)(2,1)S(1)}, bf16[2,1536]{1,0:T(2,128)(2,1)S(1)}, u32[]{:S(2)}, u32[]{:S(2)}) collective-permute-start(bf16[2,1536]{1,0:T(2,128)(2,1)S(1)} %get-tuple-element.109), channel_id=1, source_target_pairs={{1,0},{2,1},{3,2},{4,3},{5,4},{6,5},{7,6},{8,7},{9,8},{10,9},{11,1... | collective-permute-start | bytes 18440 | tf_op jit(solution)/shard_map/ppermute | solution.py:20
  21.3 0.9 copy-start.4
  23.3 79.4 %all-gather.3.cloned.1.call-start = ((), (), s32[]{:S(2)}) async-start(), calls=%async_computation | async-start | bytes 1114112 | tf_op jit(solution)/shard_map/all_gather | solution.py:105
  104.6 1.4 copy-start.1
  108.2 1.2 copy-start.2
  111.2 1.4 copy-start.1
  114.8 1.2 copy-start.2
  117.9 1.4 copy-start.1
  121.5 1.2 copy-start.2
  124.5 1.4 copy-start.1
  128.1 1.2 copy-start.2
  131.1 1.4 copy-start.1
  134.8 1.2 copy-start.2
  137.8 1.4 copy-start.1
  141.4 1.2 copy-start.2
  144.4 1.4 copy-start.1
  148.0 1.2 copy-start.2
  151.0 1.4 copy-start.1
  154.7 1.2 copy-start.2
  155.8 1.6 copy-start.5
  157.4 4.9 %copy-start.7 = (bf16[1536,128]{1,0:T(8,128)(2,1)S(1)}, bf16[1536,128]{1,0:T(8,128)(2,1)}, u32[]{:S(2)}) copy-start(bf16[1536,128]{1,0:T(8,128)(2,1)} %param.22) | copy-start | bytes 1179652
  157.5 5.0 %copy-start.6 = (bf16[1536,128]{1,0:T(8,128)(2,1)S(1)}, bf16[1536,128]{1,0:T(8,128)(2,1)}, u32[]{:S(2)}) copy-start(bf16[1536,128]{1,0:T(8,128)(2,1)} %param.21) | copy-start | bytes 1179652
  183.1 4.5 %collective-permute-start.2 = (bf16[1,256,128]{2,1,0:T(8,128)(2,1)S(1)}, bf16[1,256,128]{2,1,0:T(8,128)(2,1)S(1)}, u32[]{:S(2)}, u32[]{:S(2)}) collective-permute-start(bf16[1,256,128]{2,1,0:T(8,128)(2,1)S(1)} %get-tuple-element.106), channel_id=1, source_target_pairs={{0,1},{1,2},{2,3},{3,4},{4,5},{5,6},{6,7},{7,8},{8,9},{9,10},{10,1... | collective-permute-start | bytes 196616 | tf_op jit(solution)/shard_map/ppermute | solution.py:18
  185.0 5.6 %collective-permute-start.3 = (bf16[1,256,128]{2,1,0:T(8,128)(2,1)S(1)}, bf16[1,256,128]{2,1,0:T(8,128)(2,1)S(1)}, u32[]{:S(2)}, u32[]{:S(2)}) collective-permute-start(bf16[1,256,128]{2,1,0:T(8,128)(2,1)S(1)} %get-tuple-element.107), channel_id=1, source_target_pairs={{1,0},{2,1},{3,2},{4,3},{5,4},{6,5},{7,6},{8,7},{9,8},{10,9},{11,1... | collective-permute-start | bytes 196616 | tf_op jit(solution)/shard_map/ppermute | solution.py:20
  191.0 1.5 copy-start.8
Sparse Core Ops, SparseCore 0:
  23.5 39.7 all-gather.4
  65.4 37.2 all-gather.2
where the time goes:
time: 206 us; the launch traced here: 205 us
  waiting for transfers between devices  77.1 us (37%)
  matrix products  46.8 us (23%)
  local copies, waits for them, and re-layouts  20.7 us (10%)
  blocking collectives  19.7 us (10%)
  between operations  14.4 us (7%)
  other arithmetic  14.3 us (7%)
  starting transfers between devices  11 us (5%)
    all_gather x1, waiting for transfers between devices, local(): lax.all_gather(keys_local, 'seq', axis=0, tiled=True)  36.7 us
    all_gather x1, waiting for transfers between devices, local(): lax.all_gather(values_local, 'seq', axis=0, tiled=True)  34.5 us
    all_gather x1, blocking collectives, local(): right_all = lax.all_gather(right, 'seq', axis=0, tiled=True)  19.7 us
    dot_general x8, matrix products, attend_block(): jnp.einsum('hqk,kv->hqv', expo.astype(jnp.bfloat16), values_part, preferr...  17.7 us
    dot_general x8, matrix products, attend_block(): jnp.einsum('qhd,kd->hqk', queries, keys_part, preferred_element_type=jnp....  14.6 us
    while x40, local copies, waits for them, and re-layouts  14.6 us
    ppermute x2, starting transfers between devices, extended_2(): lax.ppermute(tail, axis, [(i, (i + 1) % count) for i in range(ends)])  6.45 us
    ppermute x2, waiting for transfers between devices, extended_2(): lax.ppermute(head, axis, [((i + 1) % count, i) for i in range(ends)])  5.89 us
  transfers between devices with their start and end apart: 6, of which 4 were waited for; matrix products, arithmetic and copies ran while one was open for 4% of the time, Pallas kernels for 0%

commit v1 on v0

--- a/solution.py
+++ b/solution.py
@@ -5,6 +5,28 @@
 
 HEADS = 8
 POOL = 16
+
+
+def in_order(blocks, dim):
+    blocks = jnp.moveaxis(blocks, 0, dim)
+    shape = blocks.shape
+    return blocks.reshape(*shape[:dim], shape[dim] * shape[dim + 1], *shape[dim + 2 :])
+
+
+def grow_blocks(x, axis):
+    count = lax.axis_size(axis)
+    blocks = x[None]
+    for level in range(count.bit_length() - 1):
+        bit = 1 << level
+        received = lax.ppermute(blocks, axis, [(i, i ^ bit) for i in range(count)])
+        both = jnp.stack([blocks, received])
+        upper = lax.axis_index(axis) >> level & 1
+        blocks = jnp.where(upper == 0, both, both[::-1]).reshape(-1, *x.shape)
+    return blocks
+
+
+def doubled_up(x, axis, dim):
+    return in_order(grow_blocks(x, axis), dim)
 
 
 def extended_2(cells, sides, width):
@@ -102,7 +124,7 @@
     running, totals, numer = attend_piece(
         initial,
         queries,
-        lax.all_gather(keys_local, "seq", axis=0, tiled=True),
+        doubled_up(keys_local, "seq", 0),
         lax.all_gather(values_local, "seq", axis=0, tiled=True),
     )
     result = numer / totals[..., None]

time: 206 us -> 187 us (0.908)
  waiting for transfers between devices: 77.1 us -> 45.9 us
  starting transfers between devices: 11 us -> 17.4 us
  other arithmetic: 14.3 us -> 18.9 us
  blocking collectives: 19.7 us -> 22.1 us
    ppermute x0 -> x4, waiting for transfers between devices: none -> 40 us  [grow_blocks(): received = lax.ppermute(blocks, axis, [(i, i ^ bit) for i in range(count)])]
    all_gather x1 -> x0, waiting for transfers between devices: 36.7 us -> none  [local(): lax.all_gather(keys_local, 'seq', axis=0, tiled=True)]
    all_gather x1, waiting for transfers between devices: 34.5 us -> 0.01 us  [local(): lax.all_gather(values_local, 'seq', axis=0, tiled=True)]
    ppermute x0 -> x4, starting transfers between devices: none -> 6.4 us  [grow_blocks(): received = lax.ppermute(blocks, axis, [(i, i ^ bit) for i in range(count)])]
    all_gather x1, blocking collectives: 19.7 us -> 22.1 us  [local(): right_all = lax.all_gather(right, 'seq', axis=0, tiled=True)]
    another operation x0 -> x5, other arithmetic: none -> 2.38 us  [grow_blocks(): both = jnp.stack([blocks, received])]
    select_n x0 -> x3, other arithmetic: none -> 2.16 us  [grow_blocks(): blocks = jnp.where(upper == 0, both, both[::-1]).reshape(-1, *x.shape)]
  transfers between devices with their start and end apart: 6 -> 9, of which waited for: 4 -> 6; matrix products, arithmetic and copies ran while one was open for 4% -> 5% of each run, Pallas kernels for 0% -> 0%
where the time goes in v1:
time: 187 us; the launch traced here: 186 us
  matrix products  46.2 us (25%)
  waiting for transfers between devices  45.9 us (25%)
  blocking collectives  22.1 us (12%)
  local copies, waits for them, and re-layouts  20.6 us (11%)
  other arithmetic  18.9 us (10%)
  starting transfers between devices  17.4 us (9%)
  between operations  14.4 us (8%)
    ppermute x4, waiting for transfers between devices, grow_blocks(): received = lax.ppermute(blocks, axis, [(i, i ^ bit) for i in range(count)])  40 us
    all_gather x1, blocking collectives, local(): right_all = lax.all_gather(right, 'seq', axis=0, tiled=True)  22.1 us
    dot_general x8, matrix products, attend_block(): jnp.einsum('hqk,kv->hqv', expo.astype(jnp.bfloat16), values_part, preferr...  17.6 us
    dot_general x8, matrix products, attend_block(): jnp.einsum('qhd,kd->hqk', queries, keys_part, preferred_element_type=jnp....  14.6 us
    while x40, local copies, waits for them, and re-layouts  14.5 us
    ppermute x2, starting transfers between devices, extended_2(): lax.ppermute(tail, axis, [(i, (i + 1) % count) for i in range(ends)])  6.45 us
    ppermute x4, starting transfers between devices, grow_blocks(): received = lax.ppermute(blocks, axis, [(i, i ^ bit) for i in range(count)])  6.4 us
    ppermute x2, waiting for transfers between devices, extended_2(): lax.ppermute(head, axis, [((i + 1) % count, i) for i in range(ends)])  5.89 us
  transfers between devices with their start and end apart: 9, of which 6 were waited for; matrix products, arithmetic and copies ran while one was open for 5% of the time, Pallas kernels for 0%

profile of v1, /device:TPU:1, one launch (start us, length us, event | category | flops | bytes accessed | tf_op | source)
XLA Modules:
  0.0 186.0 jit_solution(13273620033550761987)
XLA Ops:
  7.2 1.5 fusion.29
  8.8 1.4 fusion.31
  10.3 4.5 %collective-permute-start = (bf16[2,1536]{1,0:T(2,128)(2,1)S(1)}, bf16[2,1536]{1,0:T(2,128)(2,1)S(1)}, u32[]{:S(2)}, u32[]{:S(2)}) collective-permute-start(bf16[2,1536]{1,0:T(2,128)(2,1)S(1)} %get-tuple-element.108), channel_id=1, source_target_pairs={{0,1},{1,2},{2,3},{3,4},{4,5},{5,6},{6,7},{7,8},{8,9},{9,10},{10,1... | collective-permute-start | bytes 18440 | tf_op jit(solution)/shard_map/ppermute | solution.py:40
  14.8 1.9 %collective-permute-start.1 = (bf16[2,1536]{1,0:T(2,128)(2,1)S(1)}, bf16[2,1536]{1,0:T(2,128)(2,1)S(1)}, u32[]{:S(2)}, u32[]{:S(2)}) collective-permute-start(bf16[2,1536]{1,0:T(2,128)(2,1)S(1)} %get-tuple-element.109), channel_id=1, source_target_pairs={{1,0},{2,1},{3,2},{4,3},{5,4},{6,5},{7,6},{8,7},{9,8},{10,9},{11,1... | collective-permute-start | bytes 18440 | tf_op jit(solution)/shard_map/ppermute | solution.py:42
  16.8 2.9 %collective-permute-done.1 = bf16[2,1536]{1,0:T(2,128)(2,1)S(1)} collective-permute-done((bf16[2,1536]{1,0:T(2,128)(2,1)S(1)}, bf16[2,1536]{1,0:T(2,128)(2,1)S(1)}, u32[]{:S(2)}, u32[]{:S(2)}) %collective-permute-start.1) | collective-permute-done | bytes 6176 | tf_op jit(solution)/shard_map/ppermute | solution.py:42
  19.7 1.6 fusion.33
  22.2 1.1 convolution_convert_fusion.1
  23.4 1.7 convolution_convert_fusion.2
  25.1 1.2 collective-permute-done.2
  26.4 2.2 %collective-permute-start.3 = (bf16[2,256,128]{2,1,0:T(8,128)(2,1)S(1)}, bf16[2,256,128]{2,1,0:T(8,128)(2,1)S(1)}, u32[]{:S(2)}, u32[]{:S(2)}) collective-permute-start(bf16[2,256,128]{2,1,0:T(8,128)(2,1)S(1)} %get-tuple-element.111), channel_id=1, source_target_pairs={{0,2},{1,3},{2,0},{3,1},{4,6},{5,7},{6,4},{7,5},{8,10},{9,11},{10,... | collective-permute-start | bytes 393224 | tf_op jit(solution)/shard_map/ppermute | solution.py:21
  28.6 3.7 %collective-permute-done.3 = bf16[2,256,128]{2,1,0:T(8,128)(2,1)S(1)} collective-permute-done((bf16[2,256,128]{2,1,0:T(8,128)(2,1)S(1)}, bf16[2,256,128]{2,1,0:T(8,128)(2,1)S(1)}, u32[]{:S(2)}, u32[]{:S(2)}) %collective-permute-start.3) | collective-permute-done | bytes 131104 | tf_op jit(solution)/shard_map/ppermute | solution.py:21
  32.4 1.4 collective-permute-start.4
  33.8 8.5 %collective-permute-done.4 = bf16[4,256,128]{2,1,0:T(8,128)(2,1)} collective-permute-done((bf16[4,256,128]{2,1,0:T(8,128)(2,1)S(1)}, bf16[4,256,128]{2,1,0:T(8,128)(2,1)}, u32[]{:S(2)}, u32[]{:S(2)}) %collective-permute-start.4) | collective-permute-done | bytes 262176 | tf_op jit(solution)/shard_map/ppermute | solution.py:21
  44.2 2.7 %collective-permute-start.5 = (bf16[8,256,128]{2,1,0:T(8,128)(2,1)}, bf16[8,256,128]{2,1,0:T(8,128)(2,1)}, u32[]{:S(2)}, u32[]{:S(2)}) collective-permute-start(bf16[8,256,128]{2,1,0:T(8,128)(2,1)} %bitcast.10), channel_id=1, source_target_pairs={{0,8},{1,9},{2,10},{3,11},{4,12},{5,13},{6,14},{7,15},{8,0},{9,1},... | collective-permute-start | bytes 1572872 | tf_op jit(solution)/shard_map/ppermute | solution.py:21
  46.9 2.2 %fusion.39 = bf16[32,8,8,128]{3,2,1,0:T(8,128)(2,1)S(1)} fusion(bf16[1536,1024]{1,0:T(8,128)(2,1)S(1)} %copy-done, bf16[256,1536]{1,0:T(8,128)(2,1)} %copy-done.4, f32[1536]{0:T(1024)S(1)} %copy-done.11, f32[256]{0:T(256)S(1)} %add_rsqrt_fusion), kind=kOutput, calls=%fused_computation.68 | convolution fusion | flops 807141376 | bytes 4463616 | tf_op jit(solution)/shard_map/dot_general | solution.py:111
  50.0 26.6 %collective-permute-done.5 = bf16[8,256,128]{2,1,0:T(8,128)(2,1)} collective-permute-done((bf16[8,256,128]{2,1,0:T(8,128)(2,1)}, bf16[8,256,128]{2,1,0:T(8,128)(2,1)}, u32[]{:S(2)}, u32[]{:S(2)}) %collective-permute-start.5) | collective-permute-done | bytes 524320 | tf_op jit(solution)/shard_map/ppermute | solution.py:21
  76.6 1.3 pad_maximum_fusion.2
  77.9 1.2 reverse_select_fusion
  79.1 2.7 %copy.21 = bf16[24,8,8,512]{3,2,0,1:T(8,128)(2,1)} copy(bf16[24,8,8,512]{3,2,1,0:T(8,128)(2,1)} %bitcast.131) | data formatting | bytes 3145728 | tf_op jit(solution)/shard_map/reshape | solution.py:74
  81.8 53.0 %while.15 = (s32[]{:T(128)}, f32[8,256]{1,0:T(8,128)S(1)}, f32[8,256]{1,0:T(8,128)S(1)}, f32[8,256,192]{1,2,0:T(8,128)}, bf16[8,512,128]{2,1,0:T(8,128)(2,1)}, /...) while((s32[]{:T(128)}, f32[8,256]{1,0:T(8,128)S(1)}, ...), condition=%wide.region_5.6_spmd.clone, body=%wide.region_2.5_spmd.clone.sunk | while | flops 680667136 | bytes 29294768 | solution.py:79
  81.8 1.8 bitcast_reduce_fusion.2
  85.1 2.2 %fusion.104 = f32[8,256,192]{1,2,0:T(8,128)S(1)} fusion(f32[8,256,192]{1,2,0:T(8,128)S(1)} %copy-done.1, f32[512,256,8]{1,0,2:T(8,128)S(1)} %get-tuple-element.162, f32[8,256]{1,0:T(8,128)S(1)} %select_maximum_fusion.2, f32[8,256]{1,0:T(8,128)S(1)} %get-tuple-element.164, pred[]{:T(512)S(6)} %compare.44, ...), kind=kOutput, calls=%fused_computation.9.clone.1 | convolution fusion | flops 406978560 | bytes 7553029 | tf_op jit(solution)/shard_map/while/body/eval_jaxpr/hqk,kv->hqv/dot_general | solution.py:65
  87.3 1.1 copy-done.2
  88.5 1.8 bitcast_reduce_fusion.2
  91.7 2.2 %fusion.104 = f32[8,256,192]{1,2,0:T(8,128)S(1)} fusion(f32[8,256,192]{1,2,0:T(8,128)S(1)} %copy-done.1, f32[512,256,8]{1,0,2:T(8,128)S(1)} %get-tuple-element.162, f32[8,256]{1,0:T(8,128)S(1)} %select_maximum_fusion.2, f32[8,256]{1,0:T(8,128)S(1)} %get-tuple-element.164, pred[]{:T(512)S(6)} %compare.44, ...), kind=kOutput, calls=%fused_computation.9.clone.1 | convolution fusion | flops 406978560 | bytes 7553029 | tf_op jit(solution)/shard_map/while/body/eval_jaxpr/hqk,kv->hqv/dot_general | solution.py:65
  93.9 1.1 copy-done.2
  95.1 1.8 bitcast_reduce_fusion.2
  98.3 2.2 %fusion.104 = f32[8,256,192]{1,2,0:T(8,128)S(1)} fusion(f32[8,256,192]{1,2,0:T(8,128)S(1)} %copy-done.1, f32[512,256,8]{1,0,2:T(8,128)S(1)} %get-tuple-element.162, f32[8,256]{1,0:T(8,128)S(1)} %select_maximum_fusion.2, f32[8,256]{1,0:T(8,128)S(1)} %get-tuple-element.164, pred[]{:T(512)S(6)} %compare.44, ...), kind=kOutput, calls=%fused_computation.9.clone.1 | convolution fusion | flops 406978560 | bytes 7553029 | tf_op jit(solution)/shard_map/while/body/eval_jaxpr/hqk,kv->hqv/dot_general | solution.py:65
  100.6 1.1 copy-done.2
  101.7 1.8 bitcast_reduce_fusion.2
  104.9 2.2 %fusion.104 = f32[8,256,192]{1,2,0:T(8,128)S(1)} fusion(f32[8,256,192]{1,2,0:T(8,128)S(1)} %copy-done.1, f32[512,256,8]{1,0,2:T(8,128)S(1)} %get-tuple-element.162, f32[8,256]{1,0:T(8,128)S(1)} %select_maximum_fusion.2, f32[8,256]{1,0:T(8,128)S(1)} %get-tuple-element.164, pred[]{:T(512)S(6)} %compare.44, ...), kind=kOutput, calls=%fused_computation.9.clone.1 | convolution fusion | flops 406978560 | bytes 7553029 | tf_op jit(solution)/shard_map/while/body/eval_jaxpr/hqk,kv->hqv/dot_general | solution.py:65
  107.2 1.1 copy-done.2
  108.3 1.8 bitcast_reduce_fusion.2
  111.6 2.2 %fusion.104 = f32[8,256,192]{1,2,0:T(8,128)S(1)} fusion(f32[8,256,192]{1,2,0:T(8,128)S(1)} %copy-done.1, f32[512,256,8]{1,0,2:T(8,128)S(1)} %get-tuple-element.162, f32[8,256]{1,0:T(8,128)S(1)} %select_maximum_fusion.2, f32[8,256]{1,0:T(8,128)S(1)} %get-tuple-element.164, pred[]{:T(512)S(6)} %compare.44, ...), kind=kOutput, calls=%fused_computation.9.clone.1 | convolution fusion | flops 406978560 | bytes 7553029 | tf_op jit(solution)/shard_map/while/body/eval_jaxpr/hqk,kv->hqv/dot_general | solution.py:65
  114.9 1.8 bitcast_reduce_fusion.2
  118.2 2.2 %fusion.104 = f32[8,256,192]{1,2,0:T(8,128)S(1)} fusion(f32[8,256,192]{1,2,0:T(8,128)S(1)} %copy-done.1, f32[512,256,8]{1,0,2:T(8,128)S(1)} %get-tuple-element.162, f32[8,256]{1,0:T(8,128)S(1)} %select_maximum_fusion.2, f32[8,256]{1,0:T(8,128)S(1)} %get-tuple-element.164, pred[]{:T(512)S(6)} %compare.44, ...), kind=kOutput, calls=%fused_computation.9.clone.1 | convolution fusion | flops 406978560 | bytes 7553029 | tf_op jit(solution)/shard_map/while/body/eval_jaxpr/hqk,kv->hqv/dot_general | solution.py:65
  121.5 1.8 bitcast_reduce_fusion.2
  124.8 2.2 %fusion.104 = f32[8,256,192]{1,2,0:T(8,128)S(1)} fusion(f32[8,256,192]{1,2,0:T(8,128)S(1)} %copy-done.1, f32[512,256,8]{1,0,2:T(8,128)S(1)} %get-tuple-element.162, f32[8,256]{1,0:T(8,128)S(1)} %select_maximum_fusion.2, f32[8,256]{1,0:T(8,128)S(1)} %get-tuple-element.164, pred[]{:T(512)S(6)} %compare.44, ...), kind=kOutput, calls=%fused_computation.9.clone.1 | convolution fusion | flops 406978560 | bytes 7553029 | tf_op jit(solution)/shard_map/while/body/eval_jaxpr/hqk,kv->hqv/dot_general | solution.py:65
  128.2 1.8 bitcast_reduce_fusion.2
  131.4 2.2 %fusion.104 = f32[8,256,192]{1,2,0:T(8,128)S(1)} fusion(f32[8,256,192]{1,2,0:T(8,128)S(1)} %copy-done.1, f32[512,256,8]{1,0,2:T(8,128)S(1)} %get-tuple-element.162, f32[8,256]{1,0:T(8,128)S(1)} %select_maximum_fusion.2, f32[8,256]{1,0:T(8,128)S(1)} %get-tuple-element.164, pred[]{:T(512)S(6)} %compare.44, ...), kind=kOutput, calls=%fused_computation.9.clone.1 | convolution fusion | flops 406978560 | bytes 7553029 | tf_op jit(solution)/shard_map/while/body/eval_jaxpr/hqk,kv->hqv/dot_general | solution.py:65
  134.8 1.6 divide_convert_fusion
  136.4 4.8 %convert_reduce_fusion = (f32[16,1536]{1,0:T(8,128)S(1)}, bf16[256,1536]{1,0:T(8,128)(2,1)}) fusion(bf16[256,1536]{0,1:T(8,128)(2,1)S(1)} %bitcast.134, bf16[1536,1536]{1,0:T(8,128)(2,1)} %param.20, bf16[256,1536]{1,0:T(8,128)(2,1)S(1)} %copy-done.5), kind=kOutput, calls=%fused_computation.61 | convolution fusion | flops 1209901056 | bytes 7176192 | tf_op jit(solution)/shard_map/dot_general | solution.py:135
  141.6 22.1 %all_gather.7 = bf16[256,128]{1,0:T(8,128)(2,1)S(1)} all-gather(bf16[16,128]{1,0:T(8,128)(2,1)S(1)} %convolution_convert_fusion.3), channel_id=1, replica_groups=mesh['groups'=2,'seq'=16] {'seq'}, dimensions={0}, use_global_device_ids=true | all-gather | bytes 69632 | tf_op jit(solution)/shard_map/all_gather | solution.py:143
  164.5 1.9 %collective-permute-start.6 = (bf16[1,256,128]{2,1,0:T(8,128)(2,1)S(1)}, bf16[1,256,128]{2,1,0:T(8,128)(2,1)S(1)}, u32[]{:S(2)}, u32[]{:S(2)}) collective-permute-start(bf16[1,256,128]{2,1,0:T(8,128)(2,1)S(1)} %get-tuple-element.106), channel_id=1, source_target_pairs={{0,1},{1,2},{2,3},{3,4},{4,5},{5,6},{6,7},{7,8},{8,9},{9,10},{10,1... | collective-permute-start | bytes 196616 | tf_op jit(solution)/shard_map/ppermute | solution.py:40
  166.5 2.6 %collective-permute-start.7 = (bf16[1,256,128]{2,1,0:T(8,128)(2,1)S(1)}, bf16[1,256,128]{2,1,0:T(8,128)(2,1)S(1)}, u32[]{:S(2)}, u32[]{:S(2)}) collective-permute-start(bf16[1,256,128]{2,1,0:T(8,128)(2,1)S(1)} %get-tuple-element.107), channel_id=1, source_target_pairs={{1,0},{2,1},{3,2},{4,3},{5,4},{6,5},{7,6},{8,7},{9,8},{10,9},{11,1... | collective-permute-start | bytes 196616 | tf_op jit(solution)/shard_map/ppermute | solution.py:42
  169.1 3.0 %collective-permute-done.7 = bf16[1,256,128]{2,1,0:T(8,128)(2,1)S(1)} collective-permute-done((bf16[1,256,128]{2,1,0:T(8,128)(2,1)S(1)}, bf16[1,256,128]{2,1,0:T(8,128)(2,1)S(1)}, u32[]{:S(2)}, u32[]{:S(2)}) %collective-permute-start.7) | collective-permute-done | bytes 65568 | tf_op jit(solution)/shard_map/ppermute | solution.py:42
  172.4 1.5 fusion.73
  177.9 1.3 fusion.28
  (116 shorter events, 25.2 us)
Async XLA Ops:
  7.2 39.8 %copy-start = (bf16[1536,1024]{1,0:T(8,128)(2,1)S(1)}, bf16[1536,1024]{1,0:T(8,128)(2,1)}, u32[]{:S(2)}) copy-start(bf16[1536,1024]{1,0:T(8,128)(2,1)} %param.17) | copy-start | bytes 9437188
  7.2 9.5 %copy-start.9 = (f32[5,1536]{1,0:T(8,128)S(1)}, f32[5,1536]{1,0:T(8,128)}, u32[]{:S(2)}) copy-start(f32[5,1536]{1,0:T(8,128)} %param.15) | copy-start | bytes 92164
  7.2 71.9 %all-gather.2.cloned.1.call-start = ((), (), s32[]{:S(2)}) async-start(), calls=%async_computation | async-start | bytes 1671168 | tf_op jit(solution)/shard_map/all_gather | solution.py:128
  7.2 12.5 %copy-start.3 = (bf16[256,1536]{1,0:T(8,128)(2,1)S(1)}, bf16[256,1536]{1,0:T(8,128)(2,1)}, u32[]{:S(2)}) copy-start(bf16[256,1536]{1,0:T(8,128)(2,1)} %param.13) | copy-start | bytes 2359300
  8.8 13.4 %copy-start.10 = (bf16[1536,192]{0,1:T(8,128)(2,1)S(1)}, bf16[1536,192]{0,1:T(8,128)(2,1)}, u32[]{:S(2)}) copy-start(bf16[1536,192]{0,1:T(8,128)(2,1)} %param.19) | copy-start | bytes 1769476
  8.8 13.4 %copy-start.11 = (f32[1536]{0:T(1024)S(1)}, f32[1536]{0:T(1024)}, u32[]{:S(2)}) copy-start(f32[1536]{0:T(1024)} %param.16) | copy-start | bytes 18436
  10.3 6.6 %collective-permute-start = (bf16[2,1536]{1,0:T(2,128)(2,1)S(1)}, bf16[2,1536]{1,0:T(2,128)(2,1)S(1)}, u32[]{:S(2)}, u32[]{:S(2)}) collective-permute-start(bf16[2,1536]{1,0:T(2,128)(2,1)S(1)} %get-tuple-element.108), channel_id=1, source_target_pairs={{0,1},{1,2},{2,3},{3,4},{4,5},{5,6},{6,7},{7,8},{8,9},{9,10},{10,1... | collective-permute-start | bytes 18440 | tf_op jit(solution)/shard_map/ppermute | solution.py:40
  14.8 4.9 %collective-permute-start.1 = (bf16[2,1536]{1,0:T(2,128)(2,1)S(1)}, bf16[2,1536]{1,0:T(2,128)(2,1)S(1)}, u32[]{:S(2)}, u32[]{:S(2)}) collective-permute-start(bf16[2,1536]{1,0:T(2,128)(2,1)S(1)} %get-tuple-element.109), channel_id=1, source_target_pairs={{1,0},{2,1},{3,2},{4,3},{5,4},{6,5},{7,6},{8,7},{9,8},{10,9},{11,1... | collective-permute-start | bytes 18440 | tf_op jit(solution)/shard_map/ppermute | solution.py:42
  21.3 0.9 copy-start.4
  25.0 1.3 collective-permute-start.2
  26.4 5.9 %collective-permute-start.3 = (bf16[2,256,128]{2,1,0:T(8,128)(2,1)S(1)}, bf16[2,256,128]{2,1,0:T(8,128)(2,1)S(1)}, u32[]{:S(2)}, u32[]{:S(2)}) collective-permute-start(bf16[2,256,128]{2,1,0:T(8,128)(2,1)S(1)} %get-tuple-element.111), channel_id=1, source_target_pairs={{0,2},{1,3},{2,0},{3,1},{4,6},{5,7},{6,4},{7,5},{8,10},{9,11},{10,... | collective-permute-start | bytes 393224 | tf_op jit(solution)/shard_map/ppermute | solution.py:21
  32.4 9.8 %collective-permute-start.4 = (bf16[4,256,128]{2,1,0:T(8,128)(2,1)S(1)}, bf16[4,256,128]{2,1,0:T(8,128)(2,1)}, u32[]{:S(2)}, u32[]{:S(2)}) collective-permute-start(bf16[4,256,128]{2,1,0:T(8,128)(2,1)S(1)} %bitcast.132), channel_id=1, source_target_pairs={{0,4},{1,5},{2,6},{3,7},{4,0},{5,1},{6,2},{7,3},{8,12},{9,13},{10,... | collective-permute-start | bytes 786440 | tf_op jit(solution)/shard_map/ppermute | solution.py:21
  44.2 32.4 %collective-permute-start.5 = (bf16[8,256,128]{2,1,0:T(8,128)(2,1)}, bf16[8,256,128]{2,1,0:T(8,128)(2,1)}, u32[]{:S(2)}, u32[]{:S(2)}) collective-permute-start(bf16[8,256,128]{2,1,0:T(8,128)(2,1)} %bitcast.10), channel_id=1, source_target_pairs={{0,8},{1,9},{2,10},{3,11},{4,12},{5,13},{6,14},{7,15},{8,0},{9,1},... | collective-permute-start | bytes 1572872 | tf_op jit(solution)/shard_map/ppermute | solution.py:21
  83.7 1.4 copy-start.1
  87.3 1.1 copy-start.2
  90.3 1.4 copy-start.1
  93.9 1.1 copy-start.2
  96.9 1.4 copy-start.1
  100.5 1.1 copy-start.2
  103.5 1.4 copy-start.1
  107.2 1.1 copy-start.2
  110.2 1.4 copy-start.1
  113.8 1.1 copy-start.2
  116.8 1.4 copy-start.1
  120.4 1.1 copy-start.2
  123.4 1.4 copy-start.1
  127.0 1.1 copy-start.2
  130.0 1.4 copy-start.1
  133.6 1.1 copy-start.2
  134.8 1.6 copy-start.5
  136.4 4.9 %copy-start.7 = (bf16[1536,128]{1,0:T(8,128)(2,1)S(1)}, bf16[1536,128]{1,0:T(8,128)(2,1)}, u32[]{:S(2)}) copy-start(bf16[1536,128]{1,0:T(8,128)(2,1)} %param.22) | copy-start | bytes 1179652
  136.4 5.0 %copy-start.6 = (bf16[1536,128]{1,0:T(8,128)(2,1)S(1)}, bf16[1536,128]{1,0:T(8,128)(2,1)}, u32[]{:S(2)}) copy-start(bf16[1536,128]{1,0:T(8,128)(2,1)} %param.21) | copy-start | bytes 1179652
  164.5 4.5 %collective-permute-start.6 = (bf16[1,256,128]{2,1,0:T(8,128)(2,1)S(1)}, bf16[1,256,128]{2,1,0:T(8,128)(2,1)S(1)}, u32[]{:S(2)}, u32[]{:S(2)}) collective-permute-start(bf16[1,256,128]{2,1,0:T(8,128)(2,1)S(1)} %get-tuple-element.106), channel_id=1, source_target_pairs={{0,1},{1,2},{2,3},{3,4},{4,5},{5,6},{6,7},{7,8},{8,9},{9,10},{10,1... | collective-permute-start | bytes 196616 | tf_op jit(solution)/shard_map/ppermute | solution.py:40
  166.5 5.6 %collective-permute-start.7 = (bf16[1,256,128]{2,1,0:T(8,128)(2,1)S(1)}, bf16[1,256,128]{2,1,0:T(8,128)(2,1)S(1)}, u32[]{:S(2)}, u32[]{:S(2)}) collective-permute-start(bf16[1,256,128]{2,1,0:T(8,128)(2,1)S(1)} %get-tuple-element.107), channel_id=1, source_target_pairs={{1,0},{2,1},{3,2},{4,3},{5,4},{6,5},{7,6},{8,7},{9,8},{10,9},{11,1... | collective-permute-start | bytes 196616 | tf_op jit(solution)/shard_map/ppermute | solution.py:42
  172.4 1.5 copy-start.8
Sparse Core Ops, SparseCore 0:
  23.5 52.6 all-gather.1
